TPU v7x, 32 devices: a whole 2x2x4 slice. The times are simulated.
32 devices in a mesh: shard: 2 (over y), seq: 16 (over z, x, core).
Axes of the slice: x: 2, y: 2, z: 4, core: 2. Of those that a mesh axis runs over, the one named last changes fastest.
Arguments:
- queries: bfloat16 [16384, 1024], P(('shard', 'seq')), parts along dimension 0, may hold values from -112 to 112
- key_rows: bfloat16 [16384, 128], P(('shard', 'seq')), parts along dimension 0, may hold values from -4 to 4
- value_rows: bfloat16 [16384, 128], P(('shard', 'seq')), parts along dimension 0, may hold values from -6 to 6
- out_grads: bfloat16 [16384, 1024], P(('shard', 'seq')), parts along dimension 0, may hold values from -6 to 6
- segment_ids: int32 [16384], P('shard'), parts along dimension 0, may hold values from 0 to 1, never falling along the last dimension, each value on 1 to 7168 neighbouring positions
- random_blocks: int32 [128, 8, 3], P(('shard', 'seq')), parts along dimension 0, may hold values from 0 to 63, as said below
- global_blocks: int32 [4], P('shard'), parts along dimension 0, may hold values from 0 to 63
Outputs:
- attended: bfloat16 [16384, 1024], P(('shard', 'seq')), parts along dimension 0
- d_queries: bfloat16 [16384, 1024], P(('shard', 'seq')), parts along dimension 0
- d_keys: bfloat16 [16384, 128], P(('shard', 'seq')), parts along dimension 0
- d_values: bfloat16 [16384, 128], P(('shard', 'seq')), parts along dimension 0
There are 2 independent parts, one for each index of `shard`. A program takes and returns all parts, laid end to end along the dimension named above; each array names one. Nothing has to cross between parts.
Inputs may be any that keep to these rules, and one draw needn't show every extreme that they name: The 96 names of random_blocks in the rows of one device's 4 query blocks fall on at most 6 of them on any one device along seq, and on exactly 6 for some device.
All inputs are finite; a program needn't handle non-finite values.
Results may differ from a plain program's by a relative error of at most 0.035.
Values may be sent and summed in bfloat16 or wider, within the bound.
A program may use at most 128 MiB of HBM per device.

v0:
```python
import math

import jax
import jax.numpy as jnp
from jax import lax
from jax.sharding import PartitionSpec as P

HD = 128
HQ = 8
BLK = 128
RAND = 3
G = 2


masked_value = -1e30


def with_halo(array, sides, width):
    for axis, dim in sides:
        size, length = (lax.axis_size(axis), array.shape[dim])
        up = [(i, (i + 1) % size) for i in range(size - 1)]
        down = [(j, i) for i, j in up]
        last = lax.slice_in_dim(array, length - width, length, axis=dim)
        first = lax.slice_in_dim(array, 0, width, axis=dim)
        before = lax.ppermute(last, axis, up)
        after = lax.ppermute(first, axis, down)
        array = jnp.concatenate([before, array, after], axis=dim)
    return array


def spread(block, axis, owner):
    block = jnp.where(lax.axis_index(axis) == owner, block, jnp.zeros_like(block))
    return lax.psum(block, axis)


def from_behind(block, axis, distance):
    devices = range(lax.axis_size(axis))
    route = [(i - distance, i) for i in devices if i - distance in devices]
    return lax.ppermute(block, axis, route)


def routing(block_ids, per_device):
    owners = block_ids // per_device
    ordering = jnp.arange(block_ids.shape[0])
    earlier = (owners[:, None] == owners[None, :]) & (ordering[None, :] < ordering[:, None])
    return (owners, jnp.sum(earlier.astype(jnp.int32), axis=1))


def block_pass(
    query_block,
    grad_block,
    shared,
    shared_live,
    query_segs,
    shared_segs,
    random_kv,
    random_segs,
    scaling,
):
    wide = jnp.float32
    shared_mask = (query_segs[:, None, None] == shared_segs[None]) & shared_live[None, :, None]
    random_mask = query_segs[None, :, None, None] == random_segs[:, None]
    shared_scores = (
        jnp.einsum("thd,jkd->htjk", query_block, shared[:, :, :HD], preferred_element_type=wide)
        * scaling
    )
    shared_scores = jnp.where(shared_mask[None], shared_scores, masked_value)
    random_scores = (
        jnp.einsum(
            "thd,hrkd->htrk", query_block, random_kv[:, :, :, :HD], preferred_element_type=wide
        )
        * scaling
    )
    random_scores = jnp.where(random_mask, random_scores, masked_value)
    top_score = jnp.maximum(
        jnp.max(shared_scores, axis=(2, 3)), jnp.max(random_scores, axis=(2, 3))
    )
    totals = jnp.sum(jnp.exp(shared_scores - top_score[:, :, None, None]), axis=(2, 3))
    totals = totals + jnp.sum(jnp.exp(random_scores - top_score[:, :, None, None]), axis=(2, 3))
    log_totals = top_score + jnp.log(totals)
    shared_probs = jnp.exp(shared_scores - log_totals[:, :, None, None])
    random_probs = jnp.exp(random_scores - log_totals[:, :, None, None])
    shared_half = shared_probs.astype(jnp.bfloat16)
    random_half = random_probs.astype(jnp.bfloat16)
    attended = jnp.einsum(
        "htjk,jkd->thd", shared_half, shared[:, :, HD:], preferred_element_type=wide
    )
    attended = attended + jnp.einsum(
        "htrk,hrkd->thd", random_half, random_kv[:, :, :, HD:], preferred_element_type=wide
    )
    attended = attended.astype(jnp.bfloat16)
    row_dots = jnp.einsum("thd,thd->ht", grad_block, attended, preferred_element_type=wide)
    shared_dprobs = jnp.einsum(
        "thd,jkd->htjk", grad_block, shared[:, :, HD:], preferred_element_type=wide
    )
    random_dprobs = jnp.einsum(
        "thd,hrkd->htrk", grad_block, random_kv[:, :, :, HD:], preferred_element_type=wide
    )
    shared_dscores = (shared_probs * (shared_dprobs - row_dots[:, :, None, None])).astype(
        jnp.bfloat16
    )
    random_dscores = (random_probs * (random_dprobs - row_dots[:, :, None, None])).astype(
        jnp.bfloat16
    )
    query_grads = jnp.einsum(
        "htjk,jkd->thd", shared_dscores, shared[:, :, :HD], preferred_element_type=wide
    )
    query_grads = query_grads + jnp.einsum(
        "htrk,hrkd->thd", random_dscores, random_kv[:, :, :, :HD], preferred_element_type=wide
    )
    query_grads = (query_grads * scaling).astype(jnp.bfloat16)
    shared_kgrad = (
        jnp.einsum("htjk,thd->jkd", shared_dscores, query_block, preferred_element_type=wide)
        * scaling
    )
    shared_vgrad = jnp.einsum("htjk,thd->jkd", shared_half, grad_block, preferred_element_type=wide)
    shared_grads = jnp.where(
        shared_live[:, None, None], jnp.concatenate([shared_kgrad, shared_vgrad], axis=2), 0.0
    )
    random_kgrad = (
        jnp.einsum("htrk,thd->hrkd", random_dscores, query_block, preferred_element_type=wide)
        * scaling
    )
    random_vgrad = jnp.einsum(
        "htrk,thd->hrkd", random_half, grad_block, preferred_element_type=wide
    )
    random_grads = jnp.concatenate([random_kgrad, random_vgrad], axis=3)
    return (attended, query_grads, shared_grads, random_grads, log_totals, row_dots)


def body(queries, key_rows, value_rows, out_grads, segment_ids, random_blocks, global_blocks):
    scaling = 1.0 / math.sqrt(HD)
    row_count = queries.shape[0]
    qcount = row_count // BLK
    devices = lax.axis_size("seq")
    position = lax.axis_index("seq")
    total_blocks = segment_ids.shape[0] // BLK
    seg_blocks = segment_ids.reshape(total_blocks, BLK)
    joined = jnp.concatenate([key_rows, value_rows], axis=1)
    local_blocks = joined.reshape(qcount, BLK, 2 * HD)
    padded = with_halo(joined, (("seq", 0),), BLK)
    owned = global_blocks // qcount == position
    pieces = []
    for global_slot in range(G):
        picked = lax.dynamic_index_in_dim(
            local_blocks, global_blocks[global_slot] % qcount, 0, keepdims=False
        )
        pieces.append(spread(picked, "seq", global_blocks[global_slot] // qcount))
    global_kv = jnp.stack(pieces)
    chosen_ids = random_blocks.reshape(-1)
    pick_count = chosen_ids.shape[0]
    capacity = -(-pick_count // devices)
    owners, slots = routing(chosen_ids, qcount)
    outgoing_ids = (
        jnp.full((devices, capacity), -1, jnp.int32).at[owners, slots].set(chosen_ids % qcount)
    )
    wanted = lax.all_to_all(outgoing_ids, "seq", split_axis=0, concat_axis=0, tiled=True)
    wanted_clip = jnp.clip(wanted, 0, qcount - 1)
    served = local_blocks[wanted_clip]
    answer = lax.all_to_all(served, "seq", split_axis=0, concat_axis=0, tiled=True)
    random_kv = answer[owners, slots].reshape(qcount, HQ, RAND, BLK, 2 * HD)
    query_blocks = queries.reshape(qcount, BLK, HQ, HD)
    grad_blocks = out_grads.reshape(qcount, BLK, HQ, HD)

    def attend(bundle):
        block_index, query_block, grad_block, block_kv, block_ids = bundle
        global_index = position * qcount + block_index
        window = lax.dynamic_slice_in_dim(padded, block_index * BLK, 3 * BLK, 0).reshape(
            3, BLK, 2 * HD
        )
        window_ids = global_index + jnp.arange(-1, 2, dtype=jnp.int32)
        window_live = (window_ids >= 0) & (window_ids < total_blocks)
        shared_ids = jnp.concatenate([jnp.clip(window_ids, 0, total_blocks - 1), global_blocks])
        shared_live = jnp.concatenate([window_live, jnp.ones((G,), bool)])
        shared = jnp.concatenate([window, global_kv], axis=0)
        return block_pass(
            query_block,
            grad_block,
            shared,
            shared_live,
            seg_blocks[global_index],
            seg_blocks[shared_ids],
            block_kv,
            seg_blocks[block_ids],
            scaling,
        )

    attended, query_grads, shared_grads, random_grads, log_totals, row_dots = lax.map(
        attend,
        (jnp.arange(qcount, dtype=jnp.int32), query_blocks, grad_blocks, random_kv, random_blocks),
    )
    window_sum = jnp.zeros((qcount + 2, BLK, 2 * HD), jnp.float32)
    for offset in range(3):
        window_sum = window_sum.at[offset : offset + qcount].add(shared_grads[:, offset])
    from_right = from_behind(window_sum[0].astype(jnp.bfloat16), "seq", -1).astype(jnp.float32)
    from_left = from_behind(window_sum[qcount + 1].astype(jnp.bfloat16), "seq", 1).astype(
        jnp.float32
    )
    own_grads = window_sum[1 : qcount + 1]
    own_grads = own_grads.at[qcount - 1].add(from_right).at[0].add(from_left)
    global_sum = lax.psum(jnp.sum(shared_grads[:, 3:], axis=0), "seq")
    global_hits = (
        (global_blocks[:, None] % qcount == jnp.arange(qcount)[None, :]) & owned[:, None]
    ).astype(jnp.float32)
    own_grads = own_grads + jnp.einsum(
        "gq,gkd->qkd", global_hits, global_sum, precision=lax.Precision.HIGHEST
    )
    outgoing = (
        jnp.zeros((devices, capacity, BLK, 2 * HD), jnp.float32)
        .at[owners, slots]
        .set(random_grads.reshape(pick_count, BLK, 2 * HD))
    )
    returned = lax.all_to_all(outgoing, "seq", split_axis=0, concat_axis=0, tiled=True)
    request_hits = (wanted[:, :, None] == jnp.arange(qcount)[None, None, :]).astype(jnp.float32)
    own_grads = own_grads + jnp.einsum(
        "ncq,nckd->qkd", request_hits, returned, precision=lax.Precision.HIGHEST
    )
    own_flat = own_grads.reshape(row_count, 2 * HD)
    return (
        attended.reshape(row_count, HQ * HD),
        query_grads.reshape(row_count, HQ * HD),
        own_flat[:, :HD].astype(jnp.bfloat16),
        own_flat[:, HD:].astype(jnp.bfloat16),
    )


def solution(mesh):
    placed = (
        P(("shard", "seq"), None),
        P(("shard", "seq"), None),
        P(("shard", "seq"), None),
        P(("shard", "seq"), None),
        P("shard"),
        P(("shard", "seq"), None, None),
        P("shard"),
    )
    return jax.shard_map(
        body,
        mesh=mesh,
        in_specs=placed,
        out_specs=(
            P(("shard", "seq"), None),
            P(("shard", "seq"), None),
            P(("shard", "seq"), None),
            P(("shard", "seq"), None),
        ),
        check_vma=False,
    )
```

profile of v0, /device:TPU:0, one launch (start us, length us, event | category | flops | bytes accessed | tf_op | source)
XLA Modules:
  0.0 728.0 jit_solution(16399721941000266724)
XLA Ops:
  8.4 5.0 scatter_fusion
  14.1 7.4 %all-to-all-start = ((s32[16,1,6]{2,1,0:T(1,128)}), s32[16,1,6]{2,1,0:T(1,128)S(1)}, u32[]{:S(2)}, u32[]{:S(2)}) async-start(s32[16,1,6]{2,1,0:T(1,128)} %copy.205), calls=%async_computation | async-start | bytes 16384 | tf_op jit(solution)/shard_map/all_to_all | solution.py:157
  23.3 4.5 all-to-all-done
  28.0 5.9 gather_fusion.2
  33.9 4.8 all-to-all-start.1
  40.2 3.0 collective-permute-start
  53.1 101.0 %all-to-all-done.1 = bf16[16,6,128,256]{3,2,1,0:T(8,128)(2,1)} async-done(((bf16[16,6,128,256]{3,2,1,0:T(8,128)(2,1)}), bf16[16,6,128,256]{3,2,1,0:T(8,128)(2,1)}, u32[]{:S(2)}, u32[]{:S(2)}) %all-to-all-start.1) | async-done | bytes 6291488 | tf_op jit(solution)/shard_map/all_to_all | solution.py:160
  154.2 9.6 %gather_fusion.3 = bf16[96,128,256]{2,1,0:T(8,128)(2,1)} fusion(bf16[16,6,128,256]{3,2,1,0:T(8,128)(2,1)} %all-to-all-done.1, s32[96]{0:T(128)S(1)} %get-tuple-element.367), kind=kCustom, calls=%fused_computation.3 | custom fusion | bytes 12583680 | tf_op jit(solution)/shard_map/gather | solution.py:161
  163.7 61.0 %all-reduce.8.cloned.1.call-done = (bf16[1,128,256]{2,1,0:T(8,128)(2,1)}, bf16[1,128,256]{2,1,0:T(8,128)(2,1)}) async-done(((bf16[1,128,256]{2,1,0:T(8,128)(2,1)}, bf16[1,128,256]{2,1,0:T(8,128)(2,1)}), (bf16[1,128,256]{2,1,0:T(8,128)(2,1)}, bf16[1,128,256]{2,1,0:T(8,128)(2,1)})) %all-reduce.8.cloned.1.call-update) | async-done | bytes 131088 | tf_op jit(solution)/shard_map/psum | solution.py:33
  224.8 148.8 %while.23 = (s32[]{:T(128)}, bf16[4,128,8,128]{3,2,1,0:T(8,128)(2,1)}, bf16[4,128,8,128]{3,2,1,0:T(8,128)(2,1)}, f32[4,5,128,256]{2,3,1,0:T(8,128)}, f32[4,8,3,1...) while((s32[]{:T(128)}, ...), condition=%wide.region_9.10_spmd, body=%wide.region_4.9_spmd.sunk | while | flops 1627897984 | bytes 108602608 | solution.py:188
  232.8 2.1 copy.347
  234.8 2.7 dynamic-slice_bitcast_fusion.2
  255.7 2.0 maximum_bitcast_fusion.2
  257.7 2.4 copy.351
  270.0 2.1 copy.347
  272.1 2.7 dynamic-slice_bitcast_fusion.2
  294.8 2.4 copy.351
  307.2 2.1 copy.347
  309.3 2.7 dynamic-slice_bitcast_fusion.2
  330.0 2.0 maximum_bitcast_fusion.2
  332.0 2.4 copy.351
  344.4 2.1 copy.347
  346.5 2.7 dynamic-slice_bitcast_fusion.2
  369.3 2.4 copy.351
  373.6 6.1 broadcast_in_dim.99
  379.7 24.9 %scatter_fusion.1 = f32[16,6,128,256]{3,2,1,0:T(8,128)} fusion(f32[16,6,128,256]{3,2,1,0:T(8,128)} %broadcast_in_dim.99, s32[96]{0:T(128)S(1)} %fusion.66, f32[96,128,256]{2,1,0:T(8,128)} %bitcast.297), kind=kCustom, calls=%fused_computation.5 | custom fusion | bytes 37749504 | tf_op jit(solution)/shard_map/scatter | solution.py:211
  404.5 6.6 all-to-all-start.2
  411.3 2.3 copy.212
  415.4 3.0 collective-permute-start.3
  425.9 210.8 %all-to-all-done.2 = f32[16,6,128,256]{3,2,1,0:T(8,128)} async-done(((f32[16,6,128,256]{3,2,1,0:T(8,128)}), f32[16,6,128,256]{3,2,1,0:T(8,128)}, u32[]{:S(2)}, u32[]{:S(2)}) %all-to-all-start.2) | async-done | bytes 12582944 | tf_op jit(solution)/shard_map/all_to_all | solution.py:213
  636.8 15.5 %fusion.43 = f32[4,128,256]{2,0,1:T(4,128)S(1)} fusion(f32[16,6,128,256]{3,2,1,0:T(8,128)} %all-to-all-done.2, s32[16,6]{0,1:T(8,128)S(1)} %bitcast.304), kind=kOutput, calls=%fused_computation.85 | convolution fusion | flops 150995328 | bytes 13107584 | tf_op jit(solution)/shard_map/ncq,nckd->qkd/dot_general | solution.py:215
  652.3 66.3 %all-reduce.6.cloned.1.call-done = f32[2,128,256]{2,0,1:T(2,128)} async-done(((f32[2,128,256]{2,0,1:T(2,128)}), f32[2,128,256]{2,0,1:T(2,128)}) %all-reduce.6.cloned.1.call-update) | async-done | bytes 262160 | tf_op jit(solution)/shard_map/psum | solution.py:201
  (344 shorter events, 131.8 us)
Async XLA Ops:
  14.1 13.7 %all-to-all-start = ((s32[16,1,6]{2,1,0:T(1,128)}), s32[16,1,6]{2,1,0:T(1,128)S(1)}, u32[]{:S(2)}, u32[]{:S(2)}) async-start(s32[16,1,6]{2,1,0:T(1,128)} %copy.205), calls=%async_computation | async-start | bytes 16384 | tf_op jit(solution)/shard_map/all_to_all | solution.py:157
  33.9 9.3 %copy-start.16 = (s32[2]{0:T(128)S(1)}, s32[2]{0:T(128)}, u32[]{:S(2)}) copy-start(s32[2]{0:T(128)} %param.25) | copy-start | bytes 28
  33.9 15.9 %copy-start.11 = (bf16[512,1024]{1,0:T(8,128)(2,1)S(1)}, bf16[512,1024]{1,0:T(8,128)(2,1)}, u32[]{:S(2)}) copy-start(bf16[512,1024]{1,0:T(8,128)(2,1)} %param.19) | copy-start | bytes 3145732
  33.9 120.2 %all-to-all-start.1 = ((bf16[16,6,128,256]{3,2,1,0:T(8,128)(2,1)}), bf16[16,6,128,256]{3,2,1,0:T(8,128)(2,1)}, u32[]{:S(2)}, u32[]{:S(2)}) async-start(bf16[16,6,128,256]{3,2,1,0:T(8,128)(2,1)} %bitcast.294), calls=%async_computation.1 | async-start | bytes 12582912 | tf_op jit(solution)/shard_map/all_to_all | solution.py:160
  38.7 12.4 %copy-start.12 = (bf16[512,1024]{1,0:T(8,128)(2,1)S(1)}, bf16[512,1024]{1,0:T(8,128)(2,1)}, u32[]{:S(2)}) copy-start(bf16[512,1024]{1,0:T(8,128)(2,1)} %param.22) | copy-start | bytes 3145732
  38.7 186.1 %all-reduce.8.cloned.1.call-start = ((), (), s32[]{:S(2)}) async-start(), calls=%async_computation.4 | async-start | bytes 262144 | tf_op jit(solution)/shard_map/psum | solution.py:33
  38.8 13.6 %collective-permute-start.1 = (bf16[128,256]{1,0:T(8,128)(2,1)S(1)}, bf16[128,256]{1,0:T(8,128)(2,1)S(1)}, u32[]{:S(2)}, u32[]{:S(2)}) collective-permute-start(bf16[128,256]{1,0:T(8,128)(2,1)S(1)} %get-tuple-element.382), channel_id=1, source_target_pairs={{1,0},{2,1},{3,2},{4,3},{5,4},{6,5},{7,6},{8,7},{9,8},{10,9},{11,1... | collective-permute-start | bytes 196616 | tf_op jit(solution)/shard_map/ppermute | solution.py:26
  40.2 12.2 %collective-permute-start = (bf16[128,256]{1,0:T(8,128)(2,1)S(1)}, bf16[128,256]{1,0:T(8,128)(2,1)S(1)}, u32[]{:S(2)}, u32[]{:S(2)}) collective-permute-start(bf16[128,256]{1,0:T(8,128)(2,1)S(1)} %get-tuple-element.381), channel_id=1, source_target_pairs={{0,1},{1,2},{2,3},{3,4},{4,5},{5,6},{6,7},{7,8},{8,9},{9,10},{10,1... | collective-permute-start | bytes 196616 | tf_op jit(solution)/shard_map/ppermute | solution.py:25
  154.1 70.6 %copy-start.9 = (s32[8192]{0:T(1024)S(1)}, s32[8192]{0:T(1024)}, u32[]{:S(2)}) copy-start(s32[8192]{0:T(1024)} %param.23) | copy-start | bytes 98308
  224.8 4.7 copy-start.18
  230.2 4.6 copy-start.15
  240.7 4.4 copy-start
  245.1 4.5 copy-start.8
  250.5 2.5 copy-start.3
  262.0 4.7 copy-start.18
  267.4 4.6 copy-start.15
  277.9 4.4 copy-start
  282.3 4.5 copy-start.8
  299.2 4.7 copy-start.18
  304.6 4.6 copy-start.15
  315.1 4.4 copy-start
  319.5 4.5 copy-start.8
  336.4 4.7 copy-start.18
  341.8 4.6 copy-start.15
  352.3 4.4 copy-start
  356.7 4.5 copy-start.8
  404.5 232.2 %all-to-all-start.2 = ((f32[16,6,128,256]{3,2,1,0:T(8,128)}), f32[16,6,128,256]{3,2,1,0:T(8,128)}, u32[]{:S(2)}, u32[]{:S(2)}) async-start(f32[16,6,128,256]{3,2,1,0:T(8,128)} %scatter_fusion.1), calls=%async_computation.2 | async-start | bytes 25165824 | tf_op jit(solution)/shard_map/all_to_all | solution.py:213
  411.1 307.5 %all-reduce.6.cloned.1.call-start = ((), (), s32[]{:S(2)}) async-start(), calls=%async_computation.3 | async-start | bytes 524288 | tf_op jit(solution)/shard_map/psum | solution.py:201
  413.9 6.8 copy-start.13
  413.9 6.8 copy-start.14
  414.0 8.6 %collective-permute-start.2 = (bf16[128,256]{1,0:T(8,128)(2,1)S(1)}, bf16[128,256]{1,0:T(8,128)(2,1)S(1)}, u32[]{:S(2)}, u32[]{:S(2)}) collective-permute-start(bf16[128,256]{1,0:T(8,128)(2,1)S(1)} %fusion.52), channel_id=1, source_target_pairs={{1,0},{2,1},{3,2},{4,3},{5,4},{6,5},{7,6},{8,7},{9,8},{10,9},{11,1... | collective-permute-start | bytes 196616 | tf_op jit(solution)/shard_map/ppermute | solution.py:39
  415.4 8.4 %collective-permute-start.3 = (bf16[128,256]{1,0:T(8,128)(2,1)S(1)}, bf16[128,256]{1,0:T(8,128)(2,1)S(1)}, u32[]{:S(2)}, u32[]{:S(2)}) collective-permute-start(bf16[128,256]{1,0:T(8,128)(2,1)S(1)} %fusion.53), channel_id=1, source_target_pairs={{0,1},{1,2},{2,3},{3,4},{4,5},{5,6},{6,7},{7,8},{8,9},{9,10},{10,1... | collective-permute-start | bytes 196616 | tf_op jit(solution)/shard_map/ppermute | solution.py:39
  (36 other events, 60.4 us)
Sparse Core Ops, SparseCore 0:
  49.9 174.8 all-reduce.7
  420.8 297.7 all-reduce.5
where the time goes:
time: 730 us; the launch traced here: 728 us
  waiting for transfers between devices  444 us (61%)
  local copies, waits for them, and re-layouts  149 us (20%)
  matrix products  52.5 us (7%)
  other arithmetic  29.5 us (4%)
  starting transfers between devices  27.7 us (4%)
  between operations  19.7 us (3%)
    all_to_all x1, waiting for transfers between devices, body(): lax.all_to_all(outgoing, 'seq', split_axis=0, concat_axis=0, tiled=True)  211 us
    all_to_all x1, waiting for transfers between devices, body(): lax.all_to_all(served, 'seq', split_axis=0, concat_axis=0, tiled=True)  101 us
    psum x1, waiting for transfers between devices, body(): global_sum = lax.psum(jnp.sum(shared_grads[:, 3:], axis=0), 'seq')  66.3 us
    psum x1, waiting for transfers between devices, spread(): return lax.psum(block, axis)  61 us
    dynamic_update_slice x20, local copies, waits for them, and re-layouts, body(): lax.map(attend, (jnp.arange(qcount, dtype=jnp.int32), query_blocks, grad_...  36 us
    scatter x1, local copies, waits for them, and re-layouts, body(): outgoing = jnp.zeros((devices, capacity, BLK, 2 * HD), jnp.float32).at[ow...  24.9 us
    while x108, local copies, waits for them, and re-layouts  16.1 us
    dot_general x1, matrix products, body(): jnp.einsum('ncq,nckd->qkd', request_hits, returned, precision=lax.Precisi...  15.5 us
  transfers between devices with their start and end apart: 9, of which 5 were waited for; matrix products, arithmetic and copies ran while one was open for 6% of the time, Pallas kernels for 0%

commit v1 on v0

--- a/solution.py
+++ b/solution.py
@@ -3,6 +3,8 @@
 import jax
 import jax.numpy as jnp
 from jax import lax
+from jax.experimental import pallas as pl
+from jax.experimental.pallas import tpu as pltpu
 from jax.sharding import PartitionSpec as P
 
 HD = 128
@@ -224,6 +226,236 @@
     )
 
 
+SUM_TYPE = jnp.float32
+HEADS_STEP = 2
+LOG2E = 1.4426950408889634
+DENSE_BYTES = 16 * 1024 * 1024
+
+
+def attention_kernel(
+    meta_ref,
+    random_ref,
+    global_ref,
+    query_ref,
+    grad_ref,
+    kv_ref,
+    attended_ref,
+    query_grad_ref,
+    sums_ref,
+    kvt_ref,
+    acc_ref,
+    shared_acc_ref,
+):
+    wide = jnp.float32
+    half = jnp.bfloat16
+    block = pl.program_id(0)
+    group = pl.program_id(1)
+    groups = pl.num_programs(1)
+    total_blocks = kv_ref.shape[0]
+    heads = query_ref.shape[1] // HD
+    scaling = 1.0 / math.sqrt(HD)
+    boundary = meta_ref[0]
+    mine = meta_ref[1] + block
+
+    @pl.when((block == 0) & (group == 0))
+    def _():
+        @pl.loop(0, total_blocks)
+        def _(index):
+            kvt_ref[index] = kv_ref[index].T
+            acc_ref[index] = jnp.zeros((BLK, 2 * HD), wide)
+
+    @pl.when(group == 0)
+    def _():
+        shared_acc_ref[...] = jnp.zeros(shared_acc_ref.shape, wide)
+
+    shared_ids = [
+        jnp.maximum(mine - 1, 0),
+        mine,
+        jnp.minimum(mine + 1, total_blocks - 1),
+        global_ref[0],
+        global_ref[1],
+    ]
+    dead = [
+        jnp.where(mine == 0, masked_value, 0.0).astype(wide),
+        None,
+        jnp.where(mine == total_blocks - 1, masked_value, 0.0).astype(wide),
+        None,
+        None,
+    ]
+    random_ids = [
+        [random_ref[(block * groups + group) * heads * RAND + head * RAND + pick] for head in range(heads)]
+        for pick in range(RAND)
+    ]
+
+    queries = [query_ref[:, head * HD : (head + 1) * HD] for head in range(heads)]
+    grads = [grad_ref[:, head * HD : (head + 1) * HD] for head in range(heads)]
+    query_stack = jnp.concatenate(queries, axis=0)
+    grad_stack = jnp.concatenate(grads, axis=0)
+
+    def against(rows, columns):
+        return lax.dot_general(rows, columns, (((1,), (1,)), ((), ())), preferred_element_type=wide)
+
+    def product(rows, columns):
+        return jnp.dot(rows, columns, preferred_element_type=wide)
+
+    def entries(start, stack, parts):
+        tiles = [against(kv_ref[i, :, start : start + HD], stack) for i in shared_ids]
+        for names in random_ids:
+            tiles.append(
+                jnp.concatenate(
+                    [
+                        against(kv_ref[i, :, start : start + HD], part)
+                        for i, part in zip(names, parts)
+                    ],
+                    axis=1,
+                )
+            )
+        return tiles
+
+    key_row = lax.broadcasted_iota(jnp.int32, (BLK, HD), 0)
+    query_low = lax.broadcasted_iota(jnp.int32, (BLK, HD), 1) < boundary - mine * BLK
+
+    def allowed(name):
+        return (key_row < boundary - name * BLK) == query_low
+
+    scores = entries(0, query_stack, queries)
+    factor = scaling * LOG2E
+    masked = []
+    for slot, tile in enumerate(scores):
+        pieces = []
+        for head in range(heads):
+            piece = tile[:, head * BLK : (head + 1) * BLK] * factor
+            name = shared_ids[slot] if slot < 5 else random_ids[slot - 5][head]
+            piece = jnp.where(allowed(name), piece, masked_value)
+            if slot < 5 and dead[slot] is not None:
+                piece = piece + dead[slot]
+            pieces.append(piece)
+        masked.append(jnp.concatenate(pieces, axis=1))
+    top = masked[0]
+    for tile in masked[1:]:
+        top = jnp.maximum(top, tile)
+    top = jnp.max(top, axis=0, keepdims=True)
+    powers = [jnp.exp2(tile - top) for tile in masked]
+    total = powers[0]
+    for tile in powers[1:]:
+        total = total + tile
+    inverse = 1.0 / jnp.sum(total, axis=0, keepdims=True)
+    probs = [tile * inverse for tile in powers]
+    probs_half = [tile.astype(half) for tile in probs]
+
+    def gathered(start, tiles):
+        shared = product(
+            jnp.concatenate([kvt_ref[i, start : start + HD, :] for i in shared_ids], axis=1),
+            jnp.concatenate(tiles[:5], axis=0),
+        )
+        pieces = []
+        for head in range(heads):
+            names = [random_ids[pick][head] for pick in range(RAND)]
+            pieces.append(
+                product(
+                    jnp.concatenate([kvt_ref[i, start : start + HD, :] for i in names], axis=1),
+                    jnp.concatenate(
+                        [tile[:, head * BLK : (head + 1) * BLK] for tile in tiles[5:]], axis=0
+                    ),
+                )
+            )
+        return shared + jnp.concatenate(pieces, axis=1)
+
+    attended = gathered(HD, probs_half).astype(half).astype(wide)
+    grads_turned = jnp.concatenate([part.astype(wide).T for part in grads], axis=1)
+    row_dots = jnp.sum(attended * grads_turned, axis=0, keepdims=True)
+    for head in range(heads):
+        span = slice(head * BLK, (head + 1) * BLK)
+        attended_ref[:, span] = attended[:, span].T.astype(half)
+    dprobs = entries(HD, grad_stack, grads)
+    dscores = [(p * (d - row_dots)).astype(half) for p, d in zip(probs, dprobs)]
+    query_grads = gathered(0, dscores) * scaling
+    for head in range(heads):
+        span = slice(head * BLK, (head + 1) * BLK)
+        query_grad_ref[:, span] = query_grads[:, span].T.astype(half)
+    for slot in range(5):
+        shared_acc_ref[slot, :, :HD] += product(dscores[slot], query_stack)
+        shared_acc_ref[slot, :, HD:] += product(probs_half[slot], grad_stack)
+    for pick in range(RAND):
+        for head in range(heads):
+            name = random_ids[pick][head]
+            span = slice(head * BLK, (head + 1) * BLK)
+            acc_ref[name, :, :HD] += product(dscores[5 + pick][:, span], queries[head])
+            acc_ref[name, :, HD:] += product(probs_half[5 + pick][:, span], grads[head])
+
+    @pl.when(group == groups - 1)
+    def _():
+        for slot in range(5):
+            acc_ref[shared_ids[slot]] += shared_acc_ref[slot]
+
+    @pl.when((block == pl.num_programs(0) - 1) & (group == groups - 1))
+    def _():
+        @pl.loop(0, total_blocks)
+        def _(index):
+            sums_ref[index, :, :HD] = (acc_ref[index, :, :HD] * scaling).astype(sums_ref.dtype)
+            sums_ref[index, :, HD:] = acc_ref[index, :, HD:].astype(sums_ref.dtype)
+
+
+def attention_call(meta, random_ids, global_ids, queries, out_grads, kv):
+    row_count = queries.shape[0]
+    total_blocks = kv.shape[0]
+    width = HEADS_STEP * HD
+    rows = pl.BlockSpec((BLK, width), lambda b, g, *_: (b, g))
+    whole = pl.BlockSpec((total_blocks, BLK, 2 * HD), lambda b, g, *_: (0, 0, 0))
+    return pl.pallas_call(
+        attention_kernel,
+        grid_spec=pltpu.PrefetchScalarGridSpec(
+            num_scalar_prefetch=3,
+            grid=(row_count // BLK, HQ // HEADS_STEP),
+            in_specs=[rows, rows, whole],
+            out_specs=[rows, rows, whole],
+            scratch_shapes=[
+                pltpu.VMEM((total_blocks, 2 * HD, BLK), jnp.bfloat16),
+                pltpu.VMEM((total_blocks, BLK, 2 * HD), jnp.float32),
+                pltpu.VMEM((5, BLK, 2 * HD), jnp.float32),
+            ],
+        ),
+        out_shape=[
+            jax.ShapeDtypeStruct(queries.shape, jnp.bfloat16),
+            jax.ShapeDtypeStruct(queries.shape, jnp.bfloat16),
+            jax.ShapeDtypeStruct(kv.shape, SUM_TYPE),
+        ],
+        compiler_params=pltpu.CompilerParams(
+            dimension_semantics=("arbitrary", "arbitrary"),
+            vmem_limit_bytes=56 * 1024 * 1024,
+        ),
+        name="block_attention",
+    )(meta, random_ids, global_ids, queries, out_grads, kv)
+
+
+def dense_body(queries, key_rows, value_rows, out_grads, segment_ids, random_blocks, global_blocks):
+    qcount = queries.shape[0] // BLK
+    position = lax.axis_index("seq")
+    total_blocks = segment_ids.shape[0] // BLK
+    joined = jnp.concatenate([key_rows, value_rows], axis=1)
+    kv = lax.all_gather(joined, "seq", axis=0, tiled=True).reshape(total_blocks, BLK, 2 * HD)
+    boundary = jnp.sum((segment_ids == segment_ids[0]).astype(jnp.int32))
+    meta = jnp.stack([boundary, (position * qcount).astype(jnp.int32)])
+    attended, query_grads, sums = attention_call(
+        meta, random_blocks.reshape(-1), global_blocks, queries, out_grads, kv
+    )
+    own = lax.psum_scatter(
+        sums.reshape(total_blocks * BLK, 2 * HD), "seq", scatter_dimension=0, tiled=True
+    )
+    return (
+        attended,
+        query_grads,
+        own[:, :HD].astype(jnp.bfloat16),
+        own[:, HD:].astype(jnp.bfloat16),
+    )
+
+
+def plan(*arrays):
+    tokens = arrays[4].shape[0]
+    chosen = dense_body if tokens * 2 * HD * 4 <= DENSE_BYTES else body
+    return chosen(*arrays)
+
+
 def solution(mesh):
     placed = (
         P(("shard", "seq"), None),
@@ -235,7 +467,7 @@
         P("shard"),
     )
     return jax.shard_map(
-        body,
+        plan,
         mesh=mesh,
         in_specs=placed,
         out_specs=(

time: 730 us -> 214 us (0.29)
  waiting for transfers between devices: 444 us -> 152 us
  local copies, waits for them, and re-layouts: 149 us -> 3.39 us
  matrix products: 52.5 us -> 0 us
  Pallas kernels: 0 us -> 37.3 us
  starting transfers between devices: 27.7 us -> 0.08 us
  other arithmetic: 29.5 us -> 6.04 us
    all_to_all x3 -> x0, waiting for transfers between devices: 316 us -> none  [the longest x1 211 us: body(): lax.all_to_all(outgoing, 'seq', split_axis=0, concat_axis=0, tiled=True)]
    psum x2 -> x0, waiting for transfers between devices: 127 us -> none  [the longest x1 66.3 us: body(): global_sum = lax.psum(jnp.sum(shared_grads[:, 3:], axis=0), 'seq')]
    reduce_scatter x0 -> x1, waiting for transfers between devices: none -> 103 us  [dense_body(): lax.psum_scatter(sums.reshape(total_blocks * BLK, 2 * HD), 'seq', scatter...]
    dot_general x50 -> x0, matrix products: 52.5 us -> none  [the longest x1 15.5 us: body(): jnp.einsum('ncq,nckd->qkd', request_hits, returned, precision=lax.Precisi...]
    all_gather x0 -> x1, waiting for transfers between devices: none -> 49.1 us  [dense_body(): lax.all_gather(joined, 'seq', axis=0, tiled=True)]
    pallas_call x0 -> x1, Pallas kernels: none -> 37.3 us  [attention_call(): pl.pallas_call(attention_kernel, grid_spec=pltpu.PrefetchScalarGridSpec(n...]
    dynamic_update_slice x20 -> x0, local copies, waits for them, and re-layouts: 36 us -> none  [body(): lax.map(attend, (jnp.arange(qcount, dtype=jnp.int32), query_blocks, grad_...]
    scatter x2 -> x0, local copies, waits for them, and re-layouts: 29.8 us -> none  [the longest x1 24.9 us: body(): outgoing = jnp.zeros((devices, capacity, BLK, 2 * HD), jnp.float32).at[ow...]
  transfers between devices with their start and end apart: 9 -> 2, of which waited for: 5 -> 2; matrix products, arithmetic and copies ran while one was open for 6% -> 3% of each run, Pallas kernels for 0% -> 0%
where the time goes in v1:
time: 214 us; the launch traced here: 213 us
  waiting for transfers between devices  152 us (71%)
  Pallas kernels  37.3 us (17%)
  between operations  14.1 us (7%)
  other arithmetic  6.04 us (3%)
  local copies, waits for them, and re-layouts  3.39 us (2%)
    reduce_scatter x1, waiting for transfers between devices, dense_body(): lax.psum_scatter(sums.reshape(total_blocks * BLK, 2 * HD), 'seq', scatter...  103 us
    all_gather x1, waiting for transfers between devices, dense_body(): lax.all_gather(joined, 'seq', axis=0, tiled=True)  49.1 us
    pallas_call x1, Pallas kernels, attention_call(): pl.pallas_call(attention_kernel, grid_spec=pltpu.PrefetchScalarGridSpec(n...  37.3 us
  transfers between devices with their start and end apart: 2, of which 2 were waited for; matrix products, arithmetic and copies ran while one was open for 3% of the time, Pallas kernels for 0%

profile of v1, /device:TPU:0, one launch (start us, length us, event | category | flops | bytes accessed | tf_op | source)
XLA Modules:
  0.0 213.4 jit_solution(3761865884729255663)
XLA Ops:
  7.2 0.0 all-gather.2.cloned.1.call-start
  7.2 1.7 pad_maximum_fusion
  8.9 0.0 all-gather.2.cloned.1.call-update
  8.9 0.0 reduce-scatter.2.cloned.1.call-start
  9.0 1.2 slice.11
  10.2 0.8 copy.12
  11.0 0.7 reshape.17.random_ref
  11.7 2.0 convert_reduce_fusion
  13.7 1.2 pad_add_fusion.meta_ref
  14.9 49.1 %all-gather.2.cloned.1.call-done = bf16[8192,256]{1,0:T(8,128)(2,1)} async-done(((bf16[512,256]{1,0:T(8,128)(2,1)}), bf16[8192,256]{1,0:T(8,128)(2,1)}) %all-gather.2.cloned.1.call-update) | async-done | bytes 4194320 | tf_op jit(solution)/shard_map/all_gather | solution.py:436
  64.0 37.3 %block_attention.1 = (bf16[512,1024]{1,0:T(8,128)(2,1)}, bf16[512,1024]{1,0:T(8,128)(2,1)}, f32[64,128,256]{2,1,0:T(8,128)}) custom-call(s32[2]{0:T(128)} %pad_add_fusion.meta_ref, s32[96]{0:T(128)} %reshape.17.random_ref, s32[2]{0:T(128)} %global_ref.1, bf16[512,1024]{1,0:T(8,128)(2,1)} %query_ref.1, bf16[512,1024]{1,0:T(8,128)(2,1)} %grad_ref.1, ...), custom_call_target="tpu_custom_call" | custom-call | tf_op jit(solution)/shard_map/block_attention/pallas_call | solution.py:405
  101.3 0.0 reduce-scatter.2.cloned.1.call-update
  101.4 103.4 %reduce-scatter.2.cloned.1.call-done = f32[512,256]{1,0:T(8,128)} async-done(((f32[8192,256]{1,0:T(8,128)}), f32[512,256]{1,0:T(8,128)}) %reduce-scatter.2.cloned.1.call-update) | async-done | bytes 524304 | tf_op jit(solution)/shard_map/reduce_scatter | solution.py:442
  204.7 1.1 convert.4
  205.8 0.7 fusion
Async XLA Ops:
  7.2 56.9 %all-gather.2.cloned.1.call-start = ((), (), s32[]{:S(2)}) async-start(), calls=%async_computation.1 | async-start | bytes 4456448 | tf_op jit(solution)/shard_map/all_gather | solution.py:436
  8.9 195.8 %reduce-scatter.2.cloned.1.call-start = ((), (), s32[]{:S(2)}) async-start(), calls=%async_computation.2 | async-start | bytes 8912896 | tf_op jit(solution)/shard_map/reduce_scatter | solution.py:442
Sparse Core Ops, SparseCore 0:
  10.7 53.2 all-gather.1
  101.5 103.2 reduce-scatter.1

commit v2 on v1

--- a/solution.py
+++ b/solution.py
@@ -226,7 +226,7 @@
     )
 
 
-SUM_TYPE = jnp.float32
+SUM_TYPE = jnp.bfloat16
 HEADS_STEP = 2
 LOG2E = 1.4426950408889634
 DENSE_BYTES = 16 * 1024 * 1024
@@ -428,31 +428,284 @@
     )(meta, random_ids, global_ids, queries, out_grads, kv)
 
 
+LINE = 4
+SEQ = 16
+
+
+class Place:
+    def __init__(self):
+        me = lax.axis_index("seq")
+        self.me = me
+        self.core = lax.rem(me, 2)
+        self.x = lax.rem(me // 2, 2)
+        self.z = me // 4
+        self.high = self.z // 2
+        self.step = 1 - 2 * self.high
+        self.inner = jnp.where((self.z == 1) | (self.z == 2), 1, 0)
+        self.partner = self.at(self.z, self.x, 1 - self.core)
+        self.across = self.at(self.z, 1 - self.x, self.core)
+        self.onward = self.at(self.z + self.step, self.x, self.core)
+        self.outward = self.at(self.z - self.step, self.x, self.core)
+
+    def at(self, z, x, core):
+        return z * 4 + x * 2 + core
+
+
+def greet(place):
+    barrier = pltpu.get_barrier_semaphore()
+    for other in (place.partner, place.across, place.onward):
+        pl.semaphore_signal(
+            barrier, inc=1, device_id={"seq": other}, device_id_type=pl.DeviceIdType.MESH
+        )
+
+    @pl.when(place.inner == 1)
+    def _():
+        pl.semaphore_signal(
+            barrier, inc=1, device_id={"seq": place.outward}, device_id_type=pl.DeviceIdType.MESH
+        )
+
+    pl.semaphore_wait(barrier, 3 + place.inner)
+
+
+def remote(source, target, send, receive, device):
+    return pltpu.make_async_remote_copy(
+        src_ref=source,
+        dst_ref=target,
+        send_sem=send,
+        recv_sem=receive,
+        device_id={"seq": device},
+        device_id_type=pl.DeviceIdType.MESH,
+    )
+
+
+def gather_kernel(key_ref, value_ref, out_ref, zs, zr, xs, xr, cs, cr):
+    place = Place()
+    z, step, inner = place.z, place.step, place.inner
+    lines = [z, z + step - 2 * step * inner, z + step * (2 - inner), z + step * (3 - inner)]
+    mine = [place.at(line, place.x, place.core) for line in lines]
+    theirs = [place.at(line, 1 - place.x, place.core) for line in lines]
+    out_ref[place.me, :, :HD] = key_ref[...]
+    out_ref[place.me, :, HD:] = value_ref[...]
+    greet(place)
+
+    def send(slot, sends, index, receives, to, device):
+        return remote(
+            out_ref.at[slot], out_ref.at[slot], sends.at[index], receives.at[to], device
+        )
+
+    along = [send(mine[0], zs, 0, zr, 2, place.onward)]
+    edge_own = send(mine[0], zs, 0, zr, 1, place.onward)
+    out_own = send(mine[0], zs, 1, zr, 1, place.outward)
+    relays = [
+        send(mine[1], zs, 2, zr, 3, place.onward),
+        send(mine[2], zs, 3, zr, 2, place.outward),
+        send(mine[3], zs, 4, zr, 3, place.outward),
+    ]
+    arrivals = [
+        send(mine[index], zs, 0, zr, index, place.onward) for index in range(1, LINE)
+    ]
+    crossing = [send(mine[k], xs, k, xr, k, place.across) for k in range(LINE)]
+    crossed = [send(theirs[k], xs, k, xr, k, place.across) for k in range(LINE)]
+    near = [send(mine[k], cs, k, cr, k, place.partner) for k in range(LINE)]
+    far = [send(theirs[k], cs, LINE + k, cr, LINE + k, place.partner) for k in range(LINE)]
+
+    @pl.when(inner == 0)
+    def _():
+        edge_own.start()
+
+    @pl.when(inner == 1)
+    def _():
+        along[0].start()
+        out_own.start()
+
+    crossing[0].start()
+    near[0].start()
+    for k in range(1, LINE):
+        arrivals[k - 1].wait_recv()
+
+        @pl.when(inner == 1)
+        def _(k=k):
+            relays[k - 1].start()
+
+        crossing[k].start()
+        near[k].start()
+        crossed[k - 1].wait_recv()
+        far[k - 1].start()
+    crossed[LINE - 1].wait_recv()
+    far[LINE - 1].start()
+    for k in range(LINE):
+        crossing[k].wait_send()
+        near[k].wait_send()
+        far[k].wait_send()
+        other = place.at(lines[k], place.x, 1 - place.core)
+        other_far = place.at(lines[k], 1 - place.x, 1 - place.core)
+        send(other, cs, k, cr, k, place.partner).wait_recv()
+        send(other_far, cs, LINE + k, cr, LINE + k, place.partner).wait_recv()
+
+    edge_own.wait_send()
+
+    @pl.when(inner == 1)
+    def _():
+        out_own.wait_send()
+        for relay in relays:
+            relay.wait_send()
+
+
+def gather_call(keys, values):
+    rows = keys.shape[0]
+    return pl.pallas_call(
+        gather_kernel,
+        in_specs=[pl.BlockSpec(memory_space=pltpu.VMEM)] * 2,
+        out_specs=pl.BlockSpec(memory_space=pltpu.VMEM),
+        out_shape=jax.ShapeDtypeStruct((SEQ, rows, 2 * HD), keys.dtype),
+        scratch_shapes=[
+            pltpu.SemaphoreType.DMA((5,)),
+            pltpu.SemaphoreType.DMA((LINE,)),
+            pltpu.SemaphoreType.DMA((LINE,)),
+            pltpu.SemaphoreType.DMA((LINE,)),
+            pltpu.SemaphoreType.DMA((2 * LINE,)),
+            pltpu.SemaphoreType.DMA((2 * LINE,)),
+        ],
+        compiler_params=pltpu.CompilerParams(
+            collective_id=0, has_side_effects=True, vmem_limit_bytes=32 * 1024 * 1024
+        ),
+        name="gather_blocks",
+    )(keys, values)
+
+
+def scatter_kernel(
+    sums_ref, key_ref, value_ref, pair, cross_out, cross_in, line_out, line_in,
+    ps, pr, xs, xr, zs, zr,
+):
+    place = Place()
+    z, high, inner = place.z, place.high, place.inner
+    wide = jnp.float32
+    order = [3 * (1 - high), 2 - high, 1 - z + 4 * high, z]
+    greet(place)
+
+    def paired(side, k):
+        x = 1 - place.x if side == 0 else place.x
+        index = side * LINE + k
+        source = sums_ref.at[place.at(order[k], x, 1 - place.core)]
+        return remote(source, pair.at[index], ps.at[index], pr.at[index], place.partner)
+
+    pairs = [[paired(side, k) for k in range(LINE)] for side in range(2)]
+    crosses = [
+        remote(cross_out.at[k], cross_in.at[k], xs.at[k], xr.at[k], place.across)
+        for k in range(LINE)
+    ]
+
+    def hop(k, slot, device):
+        return remote(line_out.at[k], line_in.at[slot], zs.at[k], zr.at[slot], device)
+
+    for side in range(2):
+        for k in range(LINE):
+            pairs[side][k].start()
+    for k in range(LINE):
+        pairs[0][k].wait_recv()
+        kept = sums_ref[place.at(order[k], 1 - place.x, place.core)]
+        cross_out[k] = (kept.astype(wide) + pair[k].astype(wide)).astype(cross_out.dtype)
+        crosses[k].start()
+
+    def local(k):
+        kept = sums_ref[place.at(order[k], place.x, place.core)].astype(wide)
+        return kept + pair[LINE + k].astype(wide) + cross_in[k].astype(wide)
+
+    def arrived(slot):
+        hop(0, slot, place.onward).wait_recv()
+        return line_in[slot].astype(wide)
+
+    for k in range(LINE - 1):
+        pairs[1][k].wait_recv()
+        crosses[k].wait_recv()
+
+        @pl.when(inner == 0)
+        def _(k=k):
+            line_out[k] = local(k).astype(line_out.dtype)
+            hop(k, k, place.onward).start()
+
+        @pl.when(inner == 1)
+        def _(k=k):
+            total = local(k) + arrived(k if k < 2 else 3)
+            line_out[k] = total.astype(line_out.dtype)
+            if k < 2:
+                hop(k, 3 + k, place.onward).start()
+            else:
+                hop(k, 0, place.outward).start()
+
+    pairs[1][LINE - 1].wait_recv()
+    crosses[LINE - 1].wait_recv()
+
+    def finish(total):
+        key_ref[...] = total[:, :HD].astype(key_ref.dtype)
+        value_ref[...] = total[:, HD:].astype(value_ref.dtype)
+
+    @pl.when(inner == 0)
+    def _():
+        finish(local(LINE - 1) + arrived(0))
+
+    @pl.when(inner == 1)
+    def _():
+        finish(local(LINE - 1) + arrived(2) + arrived(4))
+
+    for k in range(LINE):
+        pairs[0][k].wait_send()
+        pairs[1][k].wait_send()
+        crosses[k].wait_send()
+    for k in range(LINE - 1):
+        hop(k, k, place.onward).wait_send()
+
+
+def scatter_call(sums):
+    rows = sums.shape[1]
+    half = jnp.bfloat16
+
+    def slots(count):
+        return pltpu.VMEM((count, rows, 2 * HD), half)
+
+    return pl.pallas_call(
+        scatter_kernel,
+        in_specs=[pl.BlockSpec(memory_space=pltpu.VMEM)],
+        out_specs=[pl.BlockSpec(memory_space=pltpu.VMEM)] * 2,
+        out_shape=[jax.ShapeDtypeStruct((rows, HD), half)] * 2,
+        scratch_shapes=[
+            slots(2 * LINE),
+            slots(LINE),
+            slots(LINE),
+            slots(LINE - 1),
+            slots(5),
+            pltpu.SemaphoreType.DMA((2 * LINE,)),
+            pltpu.SemaphoreType.DMA((2 * LINE,)),
+            pltpu.SemaphoreType.DMA((LINE,)),
+            pltpu.SemaphoreType.DMA((LINE,)),
+            pltpu.SemaphoreType.DMA((LINE - 1,)),
+            pltpu.SemaphoreType.DMA((5,)),
+        ],
+        compiler_params=pltpu.CompilerParams(
+            collective_id=1, has_side_effects=True, vmem_limit_bytes=40 * 1024 * 1024
+        ),
+        name="scatter_sums",
+    )(sums)
+
+
 def dense_body(queries, key_rows, value_rows, out_grads, segment_ids, random_blocks, global_blocks):
     qcount = queries.shape[0] // BLK
     position = lax.axis_index("seq")
     total_blocks = segment_ids.shape[0] // BLK
-    joined = jnp.concatenate([key_rows, value_rows], axis=1)
-    kv = lax.all_gather(joined, "seq", axis=0, tiled=True).reshape(total_blocks, BLK, 2 * HD)
+    kv = gather_call(key_rows, value_rows).reshape(total_blocks, BLK, 2 * HD)
     boundary = jnp.sum((segment_ids == segment_ids[0]).astype(jnp.int32))
     meta = jnp.stack([boundary, (position * qcount).astype(jnp.int32)])
     attended, query_grads, sums = attention_call(
         meta, random_blocks.reshape(-1), global_blocks, queries, out_grads, kv
     )
-    own = lax.psum_scatter(
-        sums.reshape(total_blocks * BLK, 2 * HD), "seq", scatter_dimension=0, tiled=True
-    )
-    return (
-        attended,
-        query_grads,
-        own[:, :HD].astype(jnp.bfloat16),
-        own[:, HD:].astype(jnp.bfloat16),
-    )
+    key_grads, value_grads = scatter_call(sums.reshape(SEQ, -1, 2 * HD))
+    return (attended, query_grads, key_grads, value_grads)
 
 
 def plan(*arrays):
     tokens = arrays[4].shape[0]
-    chosen = dense_body if tokens * 2 * HD * 4 <= DENSE_BYTES else body
+    fits = tokens * 2 * HD * 4 <= DENSE_BYTES
+    chosen = dense_body if fits and lax.axis_size("seq") == SEQ else body
     return chosen(*arrays)
 
 

time: 214 us -> 113 us (0.53)
  waiting for transfers between devices: 152 us -> 0 us
  Pallas kernels: 37.3 us -> 98.7 us
  between operations: 14.1 us -> 0.68 us
  local copies, waits for them, and re-layouts: 3.39 us -> 9.84 us
  other arithmetic: 6.04 us -> 3.27 us
    reduce_scatter x1 -> x0, waiting for transfers between devices: 103 us -> none  [dense_body(): lax.psum_scatter(sums.reshape(total_blocks * BLK, 2 * HD), 'seq', scatter...]
    pallas_call x0 -> x2, Pallas kernels: none -> 62.5 us  [the longest x1 32 us: gather_call(): pl.pallas_call(gather_kernel, in_specs=[pl.BlockSpec(memory_space=pltpu.V...]
    all_gather x1 -> x0, waiting for transfers between devices: 49.1 us -> none  [dense_body(): lax.all_gather(joined, 'seq', axis=0, tiled=True)]
    unnamed x1 -> x11, local copies, waits for them, and re-layouts: 0.78 us -> 8.02 us
  transfers between devices with their start and end apart: 2 -> 0, of which waited for: 2 -> 0; matrix products, arithmetic and copies ran while one was open for 3% -> 0% of each run, Pallas kernels for 0% -> 0%
where the time goes in v2:
time: 113 us
  Pallas kernels  98.7 us (87%)
  local copies, waits for them, and re-layouts  9.84 us (9%)
  other arithmetic  3.27 us (3%)
    pallas_call x1, Pallas kernels, attention_call(): pl.pallas_call(attention_kernel, grid_spec=pltpu.PrefetchScalarGridSpec(n...  36.2 us
    pallas_call x1, Pallas kernels, gather_call(): pl.pallas_call(gather_kernel, in_specs=[pl.BlockSpec(memory_space=pltpu.V...  32 us
    pallas_call x1, Pallas kernels, scatter_call(): pl.pallas_call(scatter_kernel, in_specs=[pl.BlockSpec(memory_space=pltpu....  30.4 us
    unnamed x11, local copies, waits for them, and re-layouts  8.02 us

profile of v2, /device:TPU:0, one launch (start us, length us, event | category | flops | bytes accessed | tf_op | source)
XLA Modules:
  0.0 112.5 jit_solution(11880690247856839641)
XLA Ops:
  0.6 1.2 %slice.3 = s32[1]{0:T(128)} slice(s32[8192]{0:T(1024)} %param.11), slice={[0:1]} | slice | bytes 8 | tf_op jit(solution)/shard_map/slice | solution.py:696
  1.8 2.0 %convert_reduce_fusion = s32[]{:T(128)} fusion(s32[8192]{0:T(1024)} %param.11, s32[]{:T(128)} %bitcast), kind=kLoop, calls=%fused_computation | loop fusion | flops 24575 | bytes 32776 | tf_op jit(solution)/shard_map/reduce_sum | solution.py:696
  3.9 1.2 %pad_add_fusion.meta_ref = s32[2]{0:T(128)} fusion(s32[1]{0:T(128)} %bitcast.2, s32[1]{0:T(128)} %bitcast.1), kind=kLoop, calls=%fused_computation.1 | loop fusion | flops 2 | bytes 16 | tf_op jit(solution)/shard_map/stack | solution.py:697
  5.1 0.8 copy.12
  5.9 0.6 reshape.17.random_ref
  6.5 0.0 copy-start.2
  6.5 0.9 copy-done.2
  7.4 0.0 copy-start.3
  7.4 0.9 copy-done.3
  8.3 32.0 %gather_blocks.1 = bf16[16,512,256]{2,1,0:T(8,128)(2,1)S(1)} custom-call(bf16[512,128]{1,0:T(8,128)(2,1)S(1)} %copy-done.2, bf16[512,128]{1,0:T(8,128)(2,1)S(1)} %copy-done.3), custom_call_target="tpu_custom_call" | custom-call | tf_op jit(solution)/shard_map/gather_blocks/pallas_call | solution.py:556
  40.4 0.0 copy-start
  40.4 1.9 %copy-done = bf16[16,512,256]{2,1,0:T(8,128)(2,1)} copy-done((bf16[16,512,256]{2,1,0:T(8,128)(2,1)}, bf16[16,512,256]{2,1,0:T(8,128)(2,1)S(1)}, u32[]{:S(2)}) %copy-start) | copy-done | bytes 4194328
  42.3 36.2 %block_attention.1 = (bf16[512,1024]{1,0:T(8,128)(2,1)}, bf16[512,1024]{1,0:T(8,128)(2,1)}, bf16[64,128,256]{2,1,0:T(8,128)(2,1)}) custom-call(s32[2]{0:T(128)} %pad_add_fusion.meta_ref, s32[96]{0:T(128)} %reshape.17.random_ref, s32[2]{0:T(128)} %global_ref.1, bf16[512,1024]{1,0:T(8,128)(2,1)} %query_ref.1, bf16[512,1024]{1,0:T(8,128)(2,1)} %grad_ref.1, ...), custom_call_target="tpu_custom_call" | custom-call | tf_op jit(solution)/shard_map/block_attention/pallas_call | solution.py:405
  78.5 0.0 copy-start.1
  78.6 2.2 %copy-done.1 = bf16[64,128,256]{2,1,0:T(8,128)(2,1)S(1)} copy-done((bf16[64,128,256]{2,1,0:T(8,128)(2,1)S(1)}, bf16[64,128,256]{2,1,0:T(8,128)(2,1)}, u32[]{:S(2)}) %copy-start.1) | copy-done | bytes 4194328
  80.7 30.4 %scatter_sums.1 = (bf16[512,128]{1,0:T(8,128)(2,1)S(1)}, bf16[512,128]{1,0:T(8,128)(2,1)S(1)}) custom-call(bf16[16,512,256]{2,1,0:T(8,128)(2,1)S(1)} %bitcast.6), custom_call_target="tpu_custom_call" | custom-call | tf_op jit(solution)/shard_map/scatter_sums/pallas_call | solution.py:666
  111.2 0.7 copy.15
  111.8 0.7 copy.16
Async XLA Ops:
  6.5 0.9 copy-start.2
  7.4 0.9 copy-start.3
  40.4 1.9 %copy-start = (bf16[16,512,256]{2,1,0:T(8,128)(2,1)}, bf16[16,512,256]{2,1,0:T(8,128)(2,1)S(1)}, u32[]{:S(2)}) copy-start(bf16[16,512,256]{2,1,0:T(8,128)(2,1)S(1)} %gather_blocks.1) | copy-start | bytes 12582916
  78.5 2.2 %copy-start.1 = (bf16[64,128,256]{2,1,0:T(8,128)(2,1)S(1)}, bf16[64,128,256]{2,1,0:T(8,128)(2,1)}, u32[]{:S(2)}) copy-start(bf16[64,128,256]{2,1,0:T(8,128)(2,1)} %get-tuple-element.11) | copy-start | bytes 12582916

commit v3 on v2

--- a/solution.py
+++ b/solution.py
@@ -227,47 +227,77 @@
 
 
 SUM_TYPE = jnp.bfloat16
-HEADS_STEP = 2
 LOG2E = 1.4426950408889634
 DENSE_BYTES = 16 * 1024 * 1024
 
 
 def attention_kernel(
-    meta_ref,
+    random_ref,
+    global_ref,
+    segment_ref,
+    query_ref,
+    grad_ref,
+    kv_ref,
+    kvt_ref,
+    attended_ref,
+    query_grad_ref,
+    sums_ref,
+    acc_ref,
+):
+    wide = jnp.float32
+    total_blocks = kv_ref.shape[0]
+    qcount = query_ref.shape[0] // BLK
+    scaling = 1.0 / math.sqrt(HD)
+    first = lax.axis_index("seq") * qcount
+    boundary = jnp.sum((segment_ref[...] == segment_ref[0:1, 0:1]).astype(jnp.int32))
+
+    @pl.loop(0, total_blocks)
+    def _(index):
+        acc_ref[index] = jnp.zeros((BLK, 2 * HD), wide)
+
+    @pl.loop(0, qcount)
+    def _(block):
+        attend_block(
+            block,
+            first + block,
+            boundary,
+            random_ref,
+            global_ref,
+            query_ref,
+            grad_ref,
+            kv_ref,
+            kvt_ref,
+            attended_ref,
+            query_grad_ref,
+            acc_ref,
+        )
+
+    @pl.loop(0, total_blocks)
+    def _(index):
+        sums_ref[index, :, :HD] = (acc_ref[index, :, :HD] * scaling).astype(sums_ref.dtype)
+        sums_ref[index, :, HD:] = acc_ref[index, :, HD:].astype(sums_ref.dtype)
+
+
+def attend_block(
+    block,
+    mine,
+    boundary,
     random_ref,
     global_ref,
     query_ref,
     grad_ref,
     kv_ref,
+    kvt_ref,
     attended_ref,
     query_grad_ref,
-    sums_ref,
-    kvt_ref,
     acc_ref,
-    shared_acc_ref,
 ):
     wide = jnp.float32
     half = jnp.bfloat16
-    block = pl.program_id(0)
-    group = pl.program_id(1)
-    groups = pl.num_programs(1)
     total_blocks = kv_ref.shape[0]
-    heads = query_ref.shape[1] // HD
+    heads = HQ
     scaling = 1.0 / math.sqrt(HD)
-    boundary = meta_ref[0]
-    mine = meta_ref[1] + block
-
-    @pl.when((block == 0) & (group == 0))
-    def _():
-        @pl.loop(0, total_blocks)
-        def _(index):
-            kvt_ref[index] = kv_ref[index].T
-            acc_ref[index] = jnp.zeros((BLK, 2 * HD), wide)
-
-    @pl.when(group == 0)
-    def _():
-        shared_acc_ref[...] = jnp.zeros(shared_acc_ref.shape, wide)
-
+    rows = pl.ds(pl.multiple_of(block * BLK, BLK), BLK)
     shared_ids = [
         jnp.maximum(mine - 1, 0),
         mine,
@@ -282,13 +312,10 @@
         None,
         None,
     ]
-    random_ids = [
-        [random_ref[(block * groups + group) * heads * RAND + head * RAND + pick] for head in range(heads)]
-        for pick in range(RAND)
-    ]
-
-    queries = [query_ref[:, head * HD : (head + 1) * HD] for head in range(heads)]
-    grads = [grad_ref[:, head * HD : (head + 1) * HD] for head in range(heads)]
+    random_ids = [[random_ref[pick, block, head] for head in range(heads)] for pick in range(RAND)]
+
+    queries = [query_ref[rows, head * HD : (head + 1) * HD] for head in range(heads)]
+    grads = [grad_ref[rows, head * HD : (head + 1) * HD] for head in range(heads)]
     query_stack = jnp.concatenate(queries, axis=0)
     grad_stack = jnp.concatenate(grads, axis=0)
 
@@ -366,16 +393,16 @@
     row_dots = jnp.sum(attended * grads_turned, axis=0, keepdims=True)
     for head in range(heads):
         span = slice(head * BLK, (head + 1) * BLK)
-        attended_ref[:, span] = attended[:, span].T.astype(half)
+        attended_ref[rows, span] = attended[:, span].T.astype(half)
     dprobs = entries(HD, grad_stack, grads)
     dscores = [(p * (d - row_dots)).astype(half) for p, d in zip(probs, dprobs)]
     query_grads = gathered(0, dscores) * scaling
     for head in range(heads):
         span = slice(head * BLK, (head + 1) * BLK)
-        query_grad_ref[:, span] = query_grads[:, span].T.astype(half)
-    for slot in range(5):
-        shared_acc_ref[slot, :, :HD] += product(dscores[slot], query_stack)
-        shared_acc_ref[slot, :, HD:] += product(probs_half[slot], grad_stack)
+        query_grad_ref[rows, span] = query_grads[:, span].T.astype(half)
+    for slot, name in enumerate(shared_ids):
+        acc_ref[name, :, :HD] += product(dscores[slot], query_stack)
+        acc_ref[name, :, HD:] += product(probs_half[slot], grad_stack)
     for pick in range(RAND):
         for head in range(heads):
             name = random_ids[pick][head]
@@ -383,51 +410,26 @@
             acc_ref[name, :, :HD] += product(dscores[5 + pick][:, span], queries[head])
             acc_ref[name, :, HD:] += product(probs_half[5 + pick][:, span], grads[head])
 
-    @pl.when(group == groups - 1)
-    def _():
-        for slot in range(5):
-            acc_ref[shared_ids[slot]] += shared_acc_ref[slot]
-
-    @pl.when((block == pl.num_programs(0) - 1) & (group == groups - 1))
-    def _():
-        @pl.loop(0, total_blocks)
-        def _(index):
-            sums_ref[index, :, :HD] = (acc_ref[index, :, :HD] * scaling).astype(sums_ref.dtype)
-            sums_ref[index, :, HD:] = acc_ref[index, :, HD:].astype(sums_ref.dtype)
-
-
-def attention_call(meta, random_ids, global_ids, queries, out_grads, kv):
-    row_count = queries.shape[0]
-    total_blocks = kv.shape[0]
-    width = HEADS_STEP * HD
-    rows = pl.BlockSpec((BLK, width), lambda b, g, *_: (b, g))
-    whole = pl.BlockSpec((total_blocks, BLK, 2 * HD), lambda b, g, *_: (0, 0, 0))
+
+def attention_call(random_ids, global_ids, segments, queries, out_grads, kv, kvt):
+    vmem = pl.BlockSpec(memory_space=pltpu.VMEM)
+    smem = pl.BlockSpec(memory_space=pltpu.SMEM)
     return pl.pallas_call(
         attention_kernel,
-        grid_spec=pltpu.PrefetchScalarGridSpec(
-            num_scalar_prefetch=3,
-            grid=(row_count // BLK, HQ // HEADS_STEP),
-            in_specs=[rows, rows, whole],
-            out_specs=[rows, rows, whole],
-            scratch_shapes=[
-                pltpu.VMEM((total_blocks, 2 * HD, BLK), jnp.bfloat16),
-                pltpu.VMEM((total_blocks, BLK, 2 * HD), jnp.float32),
-                pltpu.VMEM((5, BLK, 2 * HD), jnp.float32),
-            ],
-        ),
+        in_specs=[smem, smem] + [vmem] * 5,
+        out_specs=[vmem] * 3,
+        scratch_shapes=[pltpu.VMEM(kv.shape, jnp.float32)],
         out_shape=[
             jax.ShapeDtypeStruct(queries.shape, jnp.bfloat16),
             jax.ShapeDtypeStruct(queries.shape, jnp.bfloat16),
             jax.ShapeDtypeStruct(kv.shape, SUM_TYPE),
         ],
-        compiler_params=pltpu.CompilerParams(
-            dimension_semantics=("arbitrary", "arbitrary"),
-            vmem_limit_bytes=56 * 1024 * 1024,
-        ),
+        compiler_params=pltpu.CompilerParams(vmem_limit_bytes=ATTEND_MIB * 1024 * 1024),
         name="block_attention",
-    )(meta, random_ids, global_ids, queries, out_grads, kv)
-
-
+    )(random_ids, global_ids, segments, queries, out_grads, kv, kvt)
+
+
+ATTEND_MIB = 32
 LINE = 4
 SEQ = 16
 
@@ -478,7 +480,7 @@
     )
 
 
-def gather_kernel(key_ref, value_ref, out_ref, zs, zr, xs, xr, cs, cr):
+def gather_kernel(key_ref, value_ref, out_ref, turned_ref, zs, zr, xs, xr, cs, cr):
     place = Place()
     z, step, inner = place.z, place.step, place.inner
     lines = [z, z + step - 2 * step * inner, z + step * (2 - inner), z + step * (3 - inner)]
@@ -520,6 +522,21 @@
 
     crossing[0].start()
     near[0].start()
+    pieces = key_ref.shape[0] // BLK
+
+    def turn(slot):
+        for piece in range(pieces):
+            rows = slice(piece * BLK, (piece + 1) * BLK)
+            turned_ref[slot * pieces + piece] = out_ref[slot, rows, :].T
+
+    def turn_partner(k):
+        other = place.at(lines[k], place.x, 1 - place.core)
+        other_far = place.at(lines[k], 1 - place.x, 1 - place.core)
+        send(other, cs, k, cr, k, place.partner).wait_recv()
+        turn(other)
+        send(other_far, cs, LINE + k, cr, LINE + k, place.partner).wait_recv()
+        turn(other_far)
+
     for k in range(1, LINE):
         arrivals[k - 1].wait_recv()
 
@@ -529,18 +546,22 @@
 
         crossing[k].start()
         near[k].start()
+        turn(mine[k - 1])
         crossed[k - 1].wait_recv()
         far[k - 1].start()
+        turn(theirs[k - 1])
+        if k > 1:
+            turn_partner(k - 2)
+    turn(mine[LINE - 1])
+    turn_partner(LINE - 2)
     crossed[LINE - 1].wait_recv()
     far[LINE - 1].start()
+    turn(theirs[LINE - 1])
+    turn_partner(LINE - 1)
     for k in range(LINE):
         crossing[k].wait_send()
         near[k].wait_send()
         far[k].wait_send()
-        other = place.at(lines[k], place.x, 1 - place.core)
-        other_far = place.at(lines[k], 1 - place.x, 1 - place.core)
-        send(other, cs, k, cr, k, place.partner).wait_recv()
-        send(other_far, cs, LINE + k, cr, LINE + k, place.partner).wait_recv()
 
     edge_own.wait_send()
 
@@ -556,8 +577,11 @@
     return pl.pallas_call(
         gather_kernel,
         in_specs=[pl.BlockSpec(memory_space=pltpu.VMEM)] * 2,
-        out_specs=pl.BlockSpec(memory_space=pltpu.VMEM),
-        out_shape=jax.ShapeDtypeStruct((SEQ, rows, 2 * HD), keys.dtype),
+        out_specs=[pl.BlockSpec(memory_space=pltpu.VMEM)] * 2,
+        out_shape=[
+            jax.ShapeDtypeStruct((SEQ, rows, 2 * HD), keys.dtype),
+            jax.ShapeDtypeStruct((SEQ * rows // BLK, 2 * HD, BLK), keys.dtype),
+        ],
         scratch_shapes=[
             pltpu.SemaphoreType.DMA((5,)),
             pltpu.SemaphoreType.DMA((LINE,)),
@@ -689,14 +713,12 @@
 
 
 def dense_body(queries, key_rows, value_rows, out_grads, segment_ids, random_blocks, global_blocks):
-    qcount = queries.shape[0] // BLK
-    position = lax.axis_index("seq")
     total_blocks = segment_ids.shape[0] // BLK
-    kv = gather_call(key_rows, value_rows).reshape(total_blocks, BLK, 2 * HD)
-    boundary = jnp.sum((segment_ids == segment_ids[0]).astype(jnp.int32))
-    meta = jnp.stack([boundary, (position * qcount).astype(jnp.int32)])
+    kv, kvt = gather_call(key_rows, value_rows)
+    kv = kv.reshape(total_blocks, BLK, 2 * HD)
     attended, query_grads, sums = attention_call(
-        meta, random_blocks.reshape(-1), global_blocks, queries, out_grads, kv
+        random_blocks.transpose(2, 0, 1), global_blocks, segment_ids.reshape(total_blocks, BLK), queries,
+        out_grads, kv, kvt,
     )
     key_grads, value_grads = scatter_call(sums.reshape(SEQ, -1, 2 * HD))
     return (attended, query_grads, key_grads, value_grads)

time: 113 us -> 94 us (0.83)
  Pallas kernels: 98.7 us -> 85.4 us
  other arithmetic: 3.27 us -> 0 us
  local copies, waits for them, and re-layouts: 9.84 us -> 7.66 us
    pallas_call x1, Pallas kernels: 36.2 us -> 23 us  [attention_call(): pl.pallas_call(attention_kernel, in_specs=[smem, smem] + [vmem] * 5, out_...]
    reduce_sum x1 -> x0, other arithmetic: 2.05 us -> none  [dense_body(): boundary = jnp.sum((segment_ids == segment_ids[0]).astype(jnp.int32))]
    another operation x1 -> x0, other arithmetic: 1.23 us -> none  [dense_body(): meta = jnp.stack([boundary, (position * qcount).astype(jnp.int32)])]
    slice x1 -> x0, local copies, waits for them, and re-layouts: 1.2 us -> none  [dense_body(): boundary = jnp.sum((segment_ids == segment_ids[0]).astype(jnp.int32))]
    unnamed x11 -> x16, local copies, waits for them, and re-layouts: 8.02 us -> 7.66 us
where the time goes in v3:
time: 94 us; the launch traced here: 93.7 us
  Pallas kernels  85.4 us (91%)
  local copies, waits for them, and re-layouts  7.66 us (8%)
    pallas_call x1, Pallas kernels, gather_call(): pl.pallas_call(gather_kernel, in_specs=[pl.BlockSpec(memory_space=pltpu.V...  31.9 us
    pallas_call x1, Pallas kernels, scatter_call(): pl.pallas_call(scatter_kernel, in_specs=[pl.BlockSpec(memory_space=pltpu....  30.6 us
    pallas_call x1, Pallas kernels, attention_call(): pl.pallas_call(attention_kernel, in_specs=[smem, smem] + [vmem] * 5, out_...  23 us
    unnamed x16, local copies, waits for them, and re-layouts  7.66 us

profile of v3, /device:TPU:0, one launch (start us, length us, event | category | flops | bytes accessed | tf_op | source)
XLA Modules:
  0.0 93.7 jit_solution(216434926680364708)
XLA Ops:
  0.6 0.0 copy-start.2
  0.6 0.9 copy-done.2
  1.5 0.0 copy-start.3
  1.5 0.9 copy-done.3
  2.4 31.9 %gather_blocks.1 = (bf16[16,512,256]{2,1,0:T(8,128)(2,1)S(1)}, bf16[64,256,128]{2,1,0:T(8,128)(2,1)S(1)}) custom-call(bf16[512,128]{1,0:T(8,128)(2,1)S(1)} %copy-done.2, bf16[512,128]{1,0:T(8,128)(2,1)S(1)} %copy-done.3), custom_call_target="tpu_custom_call" | custom-call | tf_op jit(solution)/shard_map/gather_blocks/pallas_call | solution.py:577
  34.3 0.0 copy-start
  34.3 1.2 %copy-done = bf16[512,1024]{1,0:T(8,128)(2,1)S(1)} copy-done((bf16[512,1024]{1,0:T(8,128)(2,1)S(1)}, bf16[512,1024]{1,0:T(8,128)(2,1)}, u32[]{:S(2)}) %copy-start) | copy-done | bytes 1048600
  35.5 0.0 copy-start.1
  35.5 1.2 %copy-done.1 = bf16[512,1024]{1,0:T(8,128)(2,1)S(1)} copy-done((bf16[512,1024]{1,0:T(8,128)(2,1)S(1)}, bf16[512,1024]{1,0:T(8,128)(2,1)}, u32[]{:S(2)}) %copy-start.1) | copy-done | bytes 1048600
  36.8 0.0 copy-start.4
  36.8 0.8 copy-done.4
  37.5 0.0 copy-start.5
  37.5 0.7 copy-done.5
  38.2 0.0 copy-start.6
  38.2 0.7 copy-done.6
  38.9 23.0 %block_attention.1 = (bf16[512,1024]{1,0:T(8,128)(2,1)}, bf16[512,1024]{1,0:T(8,128)(2,1)}, bf16[64,128,256]{2,1,0:T(8,128)(2,1)S(1)}) custom-call(s32[3,4,8]{2,1,0:T(4,128)S(1)} %bitcast.7, s32[2]{0:T(128)S(1)} %copy-done.6, s32[64,128]{1,0:T(8,128)S(1)} %bitcast.6, bf16[512,1024]{1,0:T(8,128)(2,1)S(1)} %copy-done, bf16[512,1024]{1,0:T(8,128)(2,1)S(1)} %copy-done.1, ...), custom_call_target="tpu_custom_call" | custom-call | tf_op jit(solution)/shard_map/block_attention/pallas_call | solution.py:417
  61.8 30.6 %scatter_sums.1 = (bf16[512,128]{1,0:T(8,128)(2,1)S(1)}, bf16[512,128]{1,0:T(8,128)(2,1)S(1)}) custom-call(bf16[16,512,256]{2,1,0:T(8,128)(2,1)S(1)} %bitcast.4), custom_call_target="tpu_custom_call" | custom-call | tf_op jit(solution)/shard_map/scatter_sums/pallas_call | solution.py:690
  92.4 0.7 copy.13
  93.0 0.7 copy.14
Async XLA Ops:
  0.6 0.9 copy-start.2
  1.5 0.9 copy-start.3
  34.3 1.2 %copy-start = (bf16[512,1024]{1,0:T(8,128)(2,1)S(1)}, bf16[512,1024]{1,0:T(8,128)(2,1)}, u32[]{:S(2)}) copy-start(bf16[512,1024]{1,0:T(8,128)(2,1)} %query_ref.1) | copy-start | bytes 3145732
  35.5 1.2 %copy-start.1 = (bf16[512,1024]{1,0:T(8,128)(2,1)S(1)}, bf16[512,1024]{1,0:T(8,128)(2,1)}, u32[]{:S(2)}) copy-start(bf16[512,1024]{1,0:T(8,128)(2,1)} %grad_ref.1) | copy-start | bytes 3145732
  36.8 0.8 copy-start.4
  37.5 0.7 copy-start.5
  38.2 0.7 copy-start.6

commit v4 on v3

--- a/solution.py
+++ b/solution.py
@@ -495,6 +495,18 @@
             out_ref.at[slot], out_ref.at[slot], sends.at[index], receives.at[to], device
         )
 
+    middle = key_ref.shape[0] // 2
+
+    def send_half(slot, start, sends, index, receives, to, device):
+        part = out_ref.at[slot, pl.ds(start, middle)]
+        return remote(part, part, sends.at[index], receives.at[to], device)
+
+    last = LINE - 1
+    detours = [
+        send_half(theirs[1], middle, zs, 5, zr, LINE, place.onward),
+        send_half(theirs[last], middle, zs, 6, zr, LINE, place.outward),
+    ]
+    detoured = send_half(theirs[last], middle, zs, 5, zr, LINE, place.onward)
     along = [send(mine[0], zs, 0, zr, 2, place.onward)]
     edge_own = send(mine[0], zs, 0, zr, 1, place.onward)
     out_own = send(mine[0], zs, 1, zr, 1, place.outward)
@@ -506,8 +518,10 @@
     arrivals = [
         send(mine[index], zs, 0, zr, index, place.onward) for index in range(1, LINE)
     ]
-    crossing = [send(mine[k], xs, k, xr, k, place.across) for k in range(LINE)]
-    crossed = [send(theirs[k], xs, k, xr, k, place.across) for k in range(LINE)]
+    crossing = [send(mine[k], xs, k, xr, k, place.across) for k in range(last)]
+    crossing.append(send_half(mine[last], 0, xs, last, xr, last, place.across))
+    crossed = [send(theirs[k], xs, k, xr, k, place.across) for k in range(last)]
+    crossed.append(send_half(theirs[last], 0, xs, last, xr, last, place.across))
     near = [send(mine[k], cs, k, cr, k, place.partner) for k in range(LINE)]
     far = [send(theirs[k], cs, LINE + k, cr, LINE + k, place.partner) for k in range(LINE)]
 
@@ -549,14 +563,27 @@
         turn(mine[k - 1])
         crossed[k - 1].wait_recv()
         far[k - 1].start()
+        if k > 1:
+
+            @pl.when(inner == 1)
+            def _(k=k):
+                if k == last:
+                    detoured.wait_recv()
+                detours[k - 2].start()
+
         turn(theirs[k - 1])
         if k > 1:
             turn_partner(k - 2)
     turn(mine[LINE - 1])
     turn_partner(LINE - 2)
-    crossed[LINE - 1].wait_recv()
-    far[LINE - 1].start()
-    turn(theirs[LINE - 1])
+    crossed[last].wait_recv()
+
+    @pl.when(inner == 0)
+    def _():
+        detoured.wait_recv()
+
+    far[last].start()
+    turn(theirs[last])
     turn_partner(LINE - 1)
     for k in range(LINE):
         crossing[k].wait_send()
@@ -568,7 +595,7 @@
     @pl.when(inner == 1)
     def _():
         out_own.wait_send()
-        for relay in relays:
+        for relay in relays + detours:
             relay.wait_send()
 
 
@@ -583,8 +610,8 @@
             jax.ShapeDtypeStruct((SEQ * rows // BLK, 2 * HD, BLK), keys.dtype),
         ],
         scratch_shapes=[
-            pltpu.SemaphoreType.DMA((5,)),
-            pltpu.SemaphoreType.DMA((LINE,)),
+            pltpu.SemaphoreType.DMA((7,)),
+            pltpu.SemaphoreType.DMA((LINE + 1,)),
             pltpu.SemaphoreType.DMA((LINE,)),
             pltpu.SemaphoreType.DMA((LINE,)),
             pltpu.SemaphoreType.DMA((2 * LINE,)),

time: 94 us -> 94 us (level)
  no operation moved by 1% of the time
where the time goes in v4:
time: 94 us; the launch traced here: 93.7 us
  Pallas kernels  85.4 us (91%)
  local copies, waits for them, and re-layouts  7.66 us (8%)
    pallas_call x1, Pallas kernels, gather_call(): pl.pallas_call(gather_kernel, in_specs=[pl.BlockSpec(memory_space=pltpu.V...  31.7 us
    pallas_call x1, Pallas kernels, scatter_call(): pl.pallas_call(scatter_kernel, in_specs=[pl.BlockSpec(memory_space=pltpu....  30.7 us
    pallas_call x1, Pallas kernels, attention_call(): pl.pallas_call(attention_kernel, in_specs=[smem, smem] + [vmem] * 5, out_...  23 us
    unnamed x16, local copies, waits for them, and re-layouts  7.66 us

profile of v4, /device:TPU:0, one launch (start us, length us, event | category | flops | bytes accessed | tf_op | source)
XLA Modules:
  0.0 93.7 jit_solution(9189673716287324334)
XLA Ops:
  0.6 0.0 copy-start.2
  0.6 0.9 copy-done.2
  1.5 0.0 copy-start.3
  1.5 0.9 copy-done.3
  2.4 31.7 %gather_blocks.1 = (bf16[16,512,256]{2,1,0:T(8,128)(2,1)S(1)}, bf16[64,256,128]{2,1,0:T(8,128)(2,1)S(1)}) custom-call(bf16[512,128]{1,0:T(8,128)(2,1)S(1)} %copy-done.2, bf16[512,128]{1,0:T(8,128)(2,1)S(1)} %copy-done.3), custom_call_target="tpu_custom_call" | custom-call | tf_op jit(solution)/shard_map/gather_blocks/pallas_call | solution.py:604
  34.2 0.0 copy-start
  34.2 1.2 %copy-done = bf16[512,1024]{1,0:T(8,128)(2,1)S(1)} copy-done((bf16[512,1024]{1,0:T(8,128)(2,1)S(1)}, bf16[512,1024]{1,0:T(8,128)(2,1)}, u32[]{:S(2)}) %copy-start) | copy-done | bytes 1048600
  35.4 0.0 copy-start.1
  35.4 1.2 %copy-done.1 = bf16[512,1024]{1,0:T(8,128)(2,1)S(1)} copy-done((bf16[512,1024]{1,0:T(8,128)(2,1)S(1)}, bf16[512,1024]{1,0:T(8,128)(2,1)}, u32[]{:S(2)}) %copy-start.1) | copy-done | bytes 1048600
  36.6 0.0 copy-start.4
  36.7 0.8 copy-done.4
  37.4 0.0 copy-start.5
  37.4 0.7 copy-done.5
  38.1 0.0 copy-start.6
  38.1 0.7 copy-done.6
  38.8 23.0 %block_attention.1 = (bf16[512,1024]{1,0:T(8,128)(2,1)}, bf16[512,1024]{1,0:T(8,128)(2,1)}, bf16[64,128,256]{2,1,0:T(8,128)(2,1)S(1)}) custom-call(s32[3,4,8]{2,1,0:T(4,128)S(1)} %bitcast.7, s32[2]{0:T(128)S(1)} %copy-done.6, s32[64,128]{1,0:T(8,128)S(1)} %bitcast.6, bf16[512,1024]{1,0:T(8,128)(2,1)S(1)} %copy-done, bf16[512,1024]{1,0:T(8,128)(2,1)S(1)} %copy-done.1, ...), custom_call_target="tpu_custom_call" | custom-call | tf_op jit(solution)/shard_map/block_attention/pallas_call | solution.py:417
  61.7 30.7 %scatter_sums.1 = (bf16[512,128]{1,0:T(8,128)(2,1)S(1)}, bf16[512,128]{1,0:T(8,128)(2,1)S(1)}) custom-call(bf16[16,512,256]{2,1,0:T(8,128)(2,1)S(1)} %bitcast.4), custom_call_target="tpu_custom_call" | custom-call | tf_op jit(solution)/shard_map/scatter_sums/pallas_call | solution.py:717
  92.4 0.7 copy.13
  93.0 0.7 copy.14
Async XLA Ops:
  0.6 0.9 copy-start.2
  1.5 0.9 copy-start.3
  34.2 1.2 %copy-start = (bf16[512,1024]{1,0:T(8,128)(2,1)S(1)}, bf16[512,1024]{1,0:T(8,128)(2,1)}, u32[]{:S(2)}) copy-start(bf16[512,1024]{1,0:T(8,128)(2,1)} %query_ref.1) | copy-start | bytes 3145732
  35.4 1.2 %copy-start.1 = (bf16[512,1024]{1,0:T(8,128)(2,1)S(1)}, bf16[512,1024]{1,0:T(8,128)(2,1)}, u32[]{:S(2)}) copy-start(bf16[512,1024]{1,0:T(8,128)(2,1)} %grad_ref.1) | copy-start | bytes 3145732
  36.6 0.8 copy-start.4
  37.4 0.7 copy-start.5
  38.1 0.7 copy-start.6
